TPU v7x, 256 devices: a whole 4x4x8 slice. The times are simulated.
256 devices in a mesh: ctx: 16 (over x_lo, z), row: 16 (over y, x_hi, core).
Axes of the slice: x: 4 (x_hi: 2, x_lo: 2; x = x_hi * 2 + x_lo), y: 4, z: 8, core: 2. Of those that a mesh axis runs over, the one named last changes fastest.
Arguments:
- queries: bfloat16 [8192, 2048], P('ctx', 'row'), may hold values from -70 to 70
- keys: bfloat16 [8192, 2048], P('ctx', 'row'), may hold values from -4 to 4
- values: bfloat16 [8192, 2048], P('ctx', 'row'), may hold values from -24 to 24
- cross_queries: bfloat16 [8192, 2048], P('ctx', 'row'), may hold values from -70 to 70
- row_keys: bfloat16 [2048, 2048], P('ctx', 'row'), may hold values from -4 to 4
- row_values: bfloat16 [2048, 2048], P('ctx', 'row'), may hold values from -24 to 24
- incidence: int32 [8192, 4], P('ctx'), may hold values from 0 to 15, as said below
- out_weight: bfloat16 [2048, 2048], P('row'), may hold values from -0.125 to 0.125
- cotangent: bfloat16 [8192, 2048], P('ctx', 'row'), may hold values from -6 to 6
Outputs:
- mixed: bfloat16 [8192, 2048], P('ctx', 'row')
- grad_queries: float32 [8192, 2048], P('ctx', 'row')
- grad_keys: float32 [8192, 2048], P('ctx', 'row')
- grad_values: float32 [8192, 2048], P('ctx', 'row')
- grad_cross_queries: float32 [8192, 2048], P('ctx', 'row')
- grad_row_keys: float32 [2048, 2048], P('ctx', 'row')
- grad_row_values: float32 [2048, 2048], P('ctx', 'row')
- grad_weight: float32 [2048, 2048], P('row', 'ctx')
Inputs may be any that keep to these rules, and one draw needn't show every extreme that they name: `incidence`: each token names 4 tiles of 128 constraint rows, repeats allowed, and attends exactly the rows of the tiles it names.
All inputs are finite; a program needn't handle non-finite values.
Results may differ from a plain program's by a relative error of at most 0.04.
Values may be sent and summed in bfloat16 or wider, within the bound.
A program may use at most 64 MiB of HBM per device.

v0:
```python
import math

import jax
import jax.numpy as jnp
from jax import lax
from jax.sharding import PartitionSpec as P

HEADS = 16
TILE = 128


block_rows = 512


def split_heads(array, local_heads):
    return array.reshape(array.shape[0], local_heads, array.shape[1] // local_heads)


def in_blocks(update, state, pieces):
    row_count = pieces[0].shape[0]
    block_count = row_count // block_rows
    stacked = tuple(
        (member.reshape((block_count, block_rows) + member.shape[1:]) for member in pieces)
    )

    def advance(current, element):
        block_index, block_parts = element
        return (update(current, block_parts, block_index * block_rows), None)

    state, unused = lax.scan(advance, state, (jnp.arange(block_count, dtype=jnp.int32), stacked))
    return state


def guarded(update, is_empty):

    def checked(state, pieces, offset):
        return lax.cond(
            is_empty(offset, pieces[0].shape[0]),
            lambda current: current,
            lambda current: update(current, pieces, offset),
            state,
        )

    return checked


def shards(
    queries, keys, values, cross_queries, row_keys, row_values, incidence, out_weight, cotangent
):
    local_heads = HEADS // lax.axis_size("row")
    seq_rows = queries.shape[0]
    head_width = queries.shape[1] // local_heads
    scaling = 1.0 / math.sqrt(head_width)
    first_row = lax.axis_index("ctx") * seq_rows
    last_row = first_row + seq_rows - 1
    query_pos = first_row + jnp.arange(seq_rows, dtype=jnp.int32)
    query_heads = split_heads(queries, local_heads)
    key_heads = split_heads(keys, local_heads)
    value_heads = split_heads(values, local_heads)
    cross_heads = split_heads(cross_queries, local_heads)

    def logits_of(queries_in, keys_in):
        return (
            jnp.einsum("qhd,khd->qhk", queries_in, keys_in, preferred_element_type=jnp.float32)
            * scaling
        )

    def causal(offset, length):
        return (offset + jnp.arange(length, dtype=jnp.int32))[None, :] <= query_pos[:, None]

    def listed(offset, length):
        tiles = (offset + jnp.arange(length, dtype=jnp.int32)) // TILE
        return jnp.any(incidence[:, :, None] == tiles[None, None, :], axis=1)

    def after_queries(offset, length):
        return offset > last_row

    def before_keys(offset, length):
        return offset + length - 1 < first_row

    def stats_update(queries_in, allow_fn):

        def update(state, pieces, offset):
            running_max, running_sum = state
            keys_in = split_heads(pieces[0], local_heads)
            allowed = allow_fn(offset, keys_in.shape[0])[:, None, :]
            logits = jnp.where(allowed, logits_of(queries_in, keys_in), -jnp.inf)
            new_max = jnp.maximum(running_max, jnp.max(logits, axis=-1))
            running_sum = running_sum * jnp.exp(running_max - new_max) + jnp.sum(
                jnp.exp(logits - new_max[:, :, None]), axis=-1
            )
            return (new_max, running_sum)

        return update

    def output_update(queries_in, log_sums, allow_fn):

        def update(accumulated, pieces, offset):
            keys_in = split_heads(pieces[0], local_heads)
            values_in = split_heads(pieces[1], local_heads)
            allowed = allow_fn(offset, keys_in.shape[0])[:, None, :]
            weights = jnp.exp(
                jnp.where(allowed, logits_of(queries_in, keys_in) - log_sums[:, :, None], -jnp.inf)
            )
            return accumulated + jnp.einsum(
                "qhk,khd->qhd",
                weights.astype(jnp.bfloat16),
                values_in,
                preferred_element_type=jnp.float32,
            )

        return update

    start_max = jnp.full((seq_rows, local_heads), -1e30, jnp.float32)
    start_sum = jnp.zeros((seq_rows, local_heads), jnp.float32)
    zero_rows = jnp.zeros((seq_rows, local_heads, head_width), jnp.float32)
    self_stats = guarded(stats_update(query_heads, causal), after_queries)
    self_max, self_sum = in_blocks(
        self_stats, (start_max, start_sum), (lax.all_gather(keys, "ctx", axis=0, tiled=True),)
    )
    self_lse = self_max + jnp.log(self_sum)
    self_output = guarded(output_update(query_heads, self_lse, causal), after_queries)
    self_out = in_blocks(
        self_output,
        zero_rows,
        (
            lax.all_gather(keys, "ctx", axis=0, tiled=True),
            lax.all_gather(values, "ctx", axis=0, tiled=True),
        ),
    )
    cross_stats = stats_update(cross_heads, listed)
    cross_max, cross_sum = in_blocks(
        cross_stats, (start_max, start_sum), (lax.all_gather(row_keys, "ctx", axis=0, tiled=True),)
    )
    cross_lse = cross_max + jnp.log(cross_sum)
    cross_output = output_update(cross_heads, cross_lse, listed)
    cross_out = in_blocks(
        cross_output,
        zero_rows,
        (
            lax.all_gather(row_keys, "ctx", axis=0, tiled=True),
            lax.all_gather(row_values, "ctx", axis=0, tiled=True),
        ),
    )
    hidden = (self_out + cross_out).astype(jnp.bfloat16).reshape(seq_rows, local_heads * head_width)
    projected = jnp.dot(hidden, out_weight, preferred_element_type=jnp.float32)
    mixed = lax.psum_scatter(projected.astype(jnp.bfloat16), "row", scatter_dimension=1, tiled=True)
    full_cotangent = lax.all_gather(cotangent, "row", axis=1, tiled=True)
    weight_partial = lax.dot_general(
        hidden, full_cotangent, (((0,), (0,)), ((), ())), preferred_element_type=jnp.float32
    )
    grad_weight = lax.psum_scatter(
        weight_partial.astype(jnp.bfloat16), "ctx", scatter_dimension=1, tiled=True
    ).astype(jnp.float32)
    grad_hidden = lax.dot_general(
        full_cotangent, out_weight, (((1,), (1,)), ((), ())), preferred_element_type=jnp.float32
    ).astype(jnp.bfloat16)
    grad_heads = split_heads(grad_hidden, local_heads)
    self_delta = jnp.sum(grad_heads.astype(jnp.float32) * self_out, axis=-1)
    cross_delta = jnp.sum(grad_heads.astype(jnp.float32) * cross_out, axis=-1)
    all_lse, all_delta = (
        lax.all_gather(self_lse, "ctx", axis=0, tiled=True),
        lax.all_gather(self_delta, "ctx", axis=0, tiled=True),
    )
    total_rows = seq_rows * lax.axis_size("ctx")

    def key_update(state, pieces, offset):
        queries_in = split_heads(pieces[0], local_heads)
        grads_in = split_heads(pieces[1], local_heads)
        length = queries_in.shape[0]
        sums_in = lax.dynamic_slice_in_dim(all_lse, offset, length, 0)
        deltas_in = lax.dynamic_slice_in_dim(all_delta, offset, length, 0)
        allowed = ((offset + jnp.arange(length, dtype=jnp.int32))[:, None] >= query_pos[None, :])[
            :, None, :
        ]
        softmax = jnp.exp(
            jnp.where(allowed, logits_of(queries_in, key_heads) - sums_in[:, :, None], -jnp.inf)
        )
        grad_vals = state[1] + jnp.einsum(
            "qhk,qhd->khd",
            softmax.astype(jnp.bfloat16),
            grads_in,
            preferred_element_type=jnp.float32,
        )
        grad_probs = jnp.einsum(
            "qhd,khd->qhk", grads_in, value_heads, preferred_element_type=jnp.float32
        )
        grad_logits = (softmax * (grad_probs - deltas_in[:, :, None])).astype(jnp.bfloat16)
        grad_keys = (
            state[0]
            + jnp.einsum(
                "qhk,qhd->khd", grad_logits, queries_in, preferred_element_type=jnp.float32
            )
            * scaling
        )
        partial_value = (
            jnp.einsum("qhk,khd->qhd", grad_logits, key_heads, preferred_element_type=jnp.float32)
            * scaling
        )
        previous = lax.dynamic_slice_in_dim(state[2], offset, length, 0)
        return (
            grad_keys,
            grad_vals,
            lax.dynamic_update_slice_in_dim(state[2], previous + partial_value, offset, 0),
        )

    key_side = guarded(key_update, before_keys)
    initial = (zero_rows, zero_rows, jnp.zeros((total_rows, local_heads, head_width), jnp.float32))
    result = in_blocks(
        key_side,
        initial,
        (
            lax.all_gather(queries, "ctx", axis=0, tiled=True),
            lax.all_gather(grad_hidden, "ctx", axis=0, tiled=True),
        ),
    )
    grad_keys = result[0]
    grad_values = result[1]
    grad_queries = lax.psum_scatter(
        result[2].astype(jnp.bfloat16), "ctx", scatter_dimension=0, tiled=True
    ).astype(jnp.float32)

    def row_update(state, pieces, offset):
        keys_in = split_heads(pieces[0], local_heads)
        values_in = split_heads(pieces[1], local_heads)
        length = keys_in.shape[0]
        allowed = listed(offset, length)[:, None, :]
        softmax = jnp.exp(
            jnp.where(allowed, logits_of(cross_heads, keys_in) - cross_lse[:, :, None], -jnp.inf)
        )
        value_part = jnp.einsum(
            "qhk,qhd->khd",
            softmax.astype(jnp.bfloat16),
            grad_heads,
            preferred_element_type=jnp.float32,
        )
        grad_probs = jnp.einsum(
            "qhd,khd->qhk", grad_heads, values_in, preferred_element_type=jnp.float32
        )
        grad_logits = (softmax * (grad_probs - cross_delta[:, :, None])).astype(jnp.bfloat16)
        grad_cross = (
            state[0]
            + jnp.einsum("qhk,khd->qhd", grad_logits, keys_in, preferred_element_type=jnp.float32)
            * scaling
        )
        key_part = (
            jnp.einsum("qhk,qhd->khd", grad_logits, cross_heads, preferred_element_type=jnp.float32)
            * scaling
        )
        previous_keys = lax.dynamic_slice_in_dim(state[1], offset, length, 0)
        previous_values = lax.dynamic_slice_in_dim(state[2], offset, length, 0)
        grad_rowkeys = lax.dynamic_update_slice_in_dim(
            state[1], previous_keys + key_part, offset, 0
        )
        grad_rowvalues = lax.dynamic_update_slice_in_dim(
            state[2], previous_values + value_part, offset, 0
        )
        return (grad_cross, grad_rowkeys, grad_rowvalues)

    all_rows = row_keys.shape[0] * lax.axis_size("ctx")
    zero_panel = jnp.zeros((all_rows, local_heads, head_width), jnp.float32)
    cross_grads = in_blocks(
        row_update,
        (zero_rows, zero_panel, zero_panel),
        (
            lax.all_gather(row_keys, "ctx", axis=0, tiled=True),
            lax.all_gather(row_values, "ctx", axis=0, tiled=True),
        ),
    )
    grad_rowkeys, grad_rowvalues = (
        lax.psum_scatter(
            cross_grads[1].astype(jnp.bfloat16), "ctx", scatter_dimension=0, tiled=True
        ).astype(jnp.float32),
        lax.psum_scatter(
            cross_grads[2].astype(jnp.bfloat16), "ctx", scatter_dimension=0, tiled=True
        ).astype(jnp.float32),
    )
    flat = local_heads * head_width
    return (
        mixed,
        grad_queries.reshape(seq_rows, flat),
        grad_keys.reshape(seq_rows, flat),
        grad_values.reshape(seq_rows, flat),
        cross_grads[0].reshape(seq_rows, flat),
        grad_rowkeys.reshape(grad_rowkeys.shape[0], flat),
        grad_rowvalues.reshape(grad_rowvalues.shape[0], flat),
        grad_weight,
    )


def solution(mesh):
    in_specs = (
        P("ctx", "row"),
        P("ctx", "row"),
        P("ctx", "row"),
        P("ctx", "row"),
        P("ctx", "row"),
        P("ctx", "row"),
        P("ctx", None),
        P("row", None),
        P("ctx", "row"),
    )
    out_specs = (
        P("ctx", "row"),
        P("ctx", "row"),
        P("ctx", "row"),
        P("ctx", "row"),
        P("ctx", "row"),
        P("ctx", "row"),
        P("ctx", "row"),
        P("row", "ctx"),
    )
    return jax.shard_map(shards, mesh=mesh, in_specs=in_specs, out_specs=out_specs, check_vma=False)
```

profile of v0, /device:TPU:8, one launch (start us, length us, event | category | flops | bytes accessed | tf_op | source)
XLA Modules:
  0.0 723.4 jit_solution(11449184660693912434)
XLA Ops:
  9.5 54.9 %all-gather.14.cloned.1.call-done = bf16[512,2048]{1,0:T(8,128)(2,1)} async-done(((bf16[512,128]{1,0:T(8,128)(2,1)}), bf16[512,2048]{1,0:T(8,128)(2,1)}) %all-gather.14.cloned.1.call-update) | async-done | bytes 2097168 | tf_op jit(solution)/shard_map/all_gather | solution.py:148
  64.4 3.1 convolution_convert_fusion.2
  68.1 36.6 %all_gather.34 = bf16[2048,128]{1,0:T(8,128)(2,1)S(1)} all-gather(bf16[128,128]{1,0:T(8,128)(2,1)S(1)} %copy-done.14), channel_id=1, replica_groups=mesh['ctx'=16,'row'=16] {'ctx'}, dimensions={0}, use_global_device_ids=true | all-gather | bytes 557056 | tf_op jit(solution)/shard_map/all_gather | solution.py:141
  104.7 11.8 %while.94 = (s32[]{:T(128)}, f32[512,1]{0,1:T(1,128)S(1)}, f32[512,1]{0,1:T(1,128)S(1)}, s32[512,4]{0,1:T(4,128)S(1)}, s32[4]{0:T(128)S(1)}, /*index=5*/bf16[4,5...) while((s32[]{:T(128)}, f32[512,1]{0,1:T(1,128)S(1)}, ...), condition=%wide.region_14.15_spmd.clone, body=%wide.region_10.14_spmd.clone.sunk | while | flops 70265344 | bytes 3446936 | solution.py:30
  116.5 34.9 %all_gather.33 = bf16[2048,128]{1,0:T(8,128)(2,1)S(1)} all-gather(bf16[128,128]{1,0:T(8,128)(2,1)S(1)} %copy-done.15), channel_id=1, replica_groups=mesh['ctx'=16,'row'=16] {'ctx'}, dimensions={0}, use_global_device_ids=true | all-gather | bytes 557056 | tf_op jit(solution)/shard_map/all_gather | solution.py:142
  151.4 11.9 %while.95 = (s32[]{:T(128)}, f32[512,1,128]{0,2,1:T(8,128)S(1)}, bf16[4,512,128]{2,1,0:T(8,128)(2,1)S(1)}, s32[512,4]{0,1:T(4,128)S(1)}, s32[4]{0:T(128)S(1)}, /...) while((s32[]{:T(128)}, f32[512,1,128]{0,2,1:T(8,128)S(1)}, ...), condition=%wide.region_17.18_spmd.clone, body=%wide.region_15.17_spmd.clone.sunk | while | flops 137240576 | bytes 1982106 | solution.py:30
  164.2 22.6 %while.92 = (s32[]{:T(128)}, f32[512,1]{0,1:T(1,128)S(1)}, f32[512,1]{0,1:T(1,128)S(1)}, s32[16]{0:T(128)S(1)}, s32[]{:T(128)}, /*index=5*/bf16[16,512,128]{2,1,...) while((s32[]{:T(128)}, f32[512,1]{0,1:T(1,128)S(1)}, ...), condition=%wide.region_5.6_spmd.clone, body=%wide.region_0.5_spmd.clone.sunk | while | flops 68683776 | bytes 2398971 | solution.py:30
  187.4 22.1 %all-gather.8.cloned.1.call-done = bf16[8192,128]{1,0:T(8,128)(2,1)} async-done(((bf16[512,128]{1,0:T(8,128)(2,1)}), bf16[8192,128]{1,0:T(8,128)(2,1)}) %all-gather.8.cloned.1.call-update) | async-done | bytes 2097168 | tf_op jit(solution)/shard_map/all_gather | solution.py:128
  210.7 33.4 %while.93 = (s32[]{:T(128)}, f32[512,1,128]{0,2,1:T(8,128)}, s32[16]{0:T(128)}, s32[]{:T(128)}, bf16[16,512,128]{2,1,0:T(8,128)(2,1)}, /*index=5*/bf16[16,512,12...) while((s32[]{:T(128)}, f32[512,1,128]{0,2,1:T(8,128)}, ...), condition=%wide.region_9.10_spmd.clone, body=%wide.region_6.9_spmd.clone.sunk | while | flops 135595008 | bytes 933107 | solution.py:30
  212.7 3.1 conditional.11
  213.3 2.5 fusion.19
  247.7 2.1 copy.60
  250.0 21.4 %while.96 = (s32[]{:T(128)}, f32[512,1,128]{0,2,1:T(8,128)}, f32[2048,1,128]{2,0,1:T(8,128)S(1)}, f32[2048,1,128]{2,0,1:T(8,128)S(1)}, bf16[4,512,128]{2,1,0:T(8...) while((s32[]{:T(128)}, f32[512,1,128]{0,2,1:T(8,128)}, ...), condition=%wide.region_28.29_spmd.clone, body=%wide.region_26.28_spmd.clone.sunk | while | flops 339615744 | bytes 10371377 | solution.py:30
  274.0 2.6 copy.58
  277.3 79.5 %all_gather.36 = f32[8192,1]{0,1:T(1,128)} all-gather(f32[512,1]{0,1:T(1,128)S(1)} %copy-done.17), channel_id=1, replica_groups=mesh['ctx'=16,'row'=16] {'ctx'}, dimensions={0}, use_global_device_ids=true | all-gather | bytes 34816 | tf_op jit(solution)/shard_map/all_gather | solution.py:162
  356.8 31.6 %all-gather.1 = f32[16,1,512]{2,1,0:T(1,128)} all-gather(f32[1,1,512]{2,1,0:T(1,128)S(1)} %bitcast.478), channel_id=2, replica_groups=mesh['ctx'=16,'row'=16] {'ctx'}, dimensions={0}, use_global_device_ids=true | all-gather | bytes 34816 | tf_op jit(solution)/shard_map/all_gather | solution.py:163
  388.4 3.2 copy.57
  391.7 2.2 broadcast_in_dim.92
  393.9 146.1 %while.97 = (s32[]{:T(128)}, f32[512,1,128]{0,2,1:T(8,128)S(1)}, f32[512,1,128]{0,2,1:T(8,128)S(1)}, f32[8192,1,128]{2,0,1:T(8,128)}, s32[16]{0:T(128)S(1)}, /*i...) while((s32[]{:T(128)}, f32[512,1,128]{0,2,1:T(8,128)S(1)}, ...), condition=%wide.region_23.24_spmd.clone.clone, body=%wide.region_20.23_spmd.clone.clone.sunk | while | flops 337970176 | bytes 7759269 | solution.py:30
  395.2 7.9 %conditional.12 = ((f32[512,1,128]{0,2,1:T(8,128)S(1)}, f32[512,1,128]{0,2,1:T(8,128)S(1)}, f32[8192,1,128]{2,0,1:T(8,128)})) conditional(s32[]{:T(128)} %convert_element_type.146, (bf16[16,512,128]{2,1,0:T(8,128)(2,1)}, s32[]{:T(128)}, s32[]{:T(128)}, s32[]{:T(128)}, bf16[512,1,128]{2,0,1:T(8,128)(2,1)S(1)}, /*index=5*/f32[8192,1]{0,1:T(1,128)}, ...), branch_computations={%region_21.21_spmd, %region_22.22_spmd} | conditional | flops 337970176 | bytes 7756894 | solution.py:37
  401.2 1.9 dynamic_update_slice.14
  404.3 7.9 %conditional.12 = ((f32[512,1,128]{0,2,1:T(8,128)S(1)}, f32[512,1,128]{0,2,1:T(8,128)S(1)}, f32[8192,1,128]{2,0,1:T(8,128)})) conditional(s32[]{:T(128)} %convert_element_type.146, (bf16[16,512,128]{2,1,0:T(8,128)(2,1)}, s32[]{:T(128)}, s32[]{:T(128)}, s32[]{:T(128)}, bf16[512,1,128]{2,0,1:T(8,128)(2,1)S(1)}, /*index=5*/f32[8192,1]{0,1:T(1,128)}, ...), branch_computations={%region_21.21_spmd, %region_22.22_spmd} | conditional | flops 337970176 | bytes 7756894 | solution.py:37
  413.5 7.9 %conditional.12 = ((f32[512,1,128]{0,2,1:T(8,128)S(1)}, f32[512,1,128]{0,2,1:T(8,128)S(1)}, f32[8192,1,128]{2,0,1:T(8,128)})) conditional(s32[]{:T(128)} %convert_element_type.146, (bf16[16,512,128]{2,1,0:T(8,128)(2,1)}, s32[]{:T(128)}, s32[]{:T(128)}, s32[]{:T(128)}, bf16[512,1,128]{2,0,1:T(8,128)(2,1)S(1)}, /*index=5*/f32[8192,1]{0,1:T(1,128)}, ...), branch_computations={%region_21.21_spmd, %region_22.22_spmd} | conditional | flops 337970176 | bytes 7756894 | solution.py:37
  419.5 1.9 dynamic_update_slice.14
  422.6 7.9 %conditional.12 = ((f32[512,1,128]{0,2,1:T(8,128)S(1)}, f32[512,1,128]{0,2,1:T(8,128)S(1)}, f32[8192,1,128]{2,0,1:T(8,128)})) conditional(s32[]{:T(128)} %convert_element_type.146, (bf16[16,512,128]{2,1,0:T(8,128)(2,1)}, s32[]{:T(128)}, s32[]{:T(128)}, s32[]{:T(128)}, bf16[512,1,128]{2,0,1:T(8,128)(2,1)S(1)}, /*index=5*/f32[8192,1]{0,1:T(1,128)}, ...), branch_computations={%region_21.21_spmd, %region_22.22_spmd} | conditional | flops 337970176 | bytes 7756894 | solution.py:37
  428.7 1.9 dynamic_update_slice.14
  431.8 7.9 %conditional.12 = ((f32[512,1,128]{0,2,1:T(8,128)S(1)}, f32[512,1,128]{0,2,1:T(8,128)S(1)}, f32[8192,1,128]{2,0,1:T(8,128)})) conditional(s32[]{:T(128)} %convert_element_type.146, (bf16[16,512,128]{2,1,0:T(8,128)(2,1)}, s32[]{:T(128)}, s32[]{:T(128)}, s32[]{:T(128)}, bf16[512,1,128]{2,0,1:T(8,128)(2,1)S(1)}, /*index=5*/f32[8192,1]{0,1:T(1,128)}, ...), branch_computations={%region_21.21_spmd, %region_22.22_spmd} | conditional | flops 337970176 | bytes 7756894 | solution.py:37
  440.9 7.9 %conditional.12 = ((f32[512,1,128]{0,2,1:T(8,128)S(1)}, f32[512,1,128]{0,2,1:T(8,128)S(1)}, f32[8192,1,128]{2,0,1:T(8,128)})) conditional(s32[]{:T(128)} %convert_element_type.146, (bf16[16,512,128]{2,1,0:T(8,128)(2,1)}, s32[]{:T(128)}, s32[]{:T(128)}, s32[]{:T(128)}, bf16[512,1,128]{2,0,1:T(8,128)(2,1)S(1)}, /*index=5*/f32[8192,1]{0,1:T(1,128)}, ...), branch_computations={%region_21.21_spmd, %region_22.22_spmd} | conditional | flops 337970176 | bytes 7756894 | solution.py:37
  446.9 1.9 dynamic_update_slice.14
  450.1 7.9 %conditional.12 = ((f32[512,1,128]{0,2,1:T(8,128)S(1)}, f32[512,1,128]{0,2,1:T(8,128)S(1)}, f32[8192,1,128]{2,0,1:T(8,128)})) conditional(s32[]{:T(128)} %convert_element_type.146, (bf16[16,512,128]{2,1,0:T(8,128)(2,1)}, s32[]{:T(128)}, s32[]{:T(128)}, s32[]{:T(128)}, bf16[512,1,128]{2,0,1:T(8,128)(2,1)S(1)}, /*index=5*/f32[8192,1]{0,1:T(1,128)}, ...), branch_computations={%region_21.21_spmd, %region_22.22_spmd} | conditional | flops 337970176 | bytes 7756894 | solution.py:37
  459.2 7.9 %conditional.12 = ((f32[512,1,128]{0,2,1:T(8,128)S(1)}, f32[512,1,128]{0,2,1:T(8,128)S(1)}, f32[8192,1,128]{2,0,1:T(8,128)})) conditional(s32[]{:T(128)} %convert_element_type.146, (bf16[16,512,128]{2,1,0:T(8,128)(2,1)}, s32[]{:T(128)}, s32[]{:T(128)}, s32[]{:T(128)}, bf16[512,1,128]{2,0,1:T(8,128)(2,1)S(1)}, /*index=5*/f32[8192,1]{0,1:T(1,128)}, ...), branch_computations={%region_21.21_spmd, %region_22.22_spmd} | conditional | flops 337970176 | bytes 7756894 | solution.py:37
  468.3 7.9 %conditional.12 = ((f32[512,1,128]{0,2,1:T(8,128)S(1)}, f32[512,1,128]{0,2,1:T(8,128)S(1)}, f32[8192,1,128]{2,0,1:T(8,128)})) conditional(s32[]{:T(128)} %convert_element_type.146, (bf16[16,512,128]{2,1,0:T(8,128)(2,1)}, s32[]{:T(128)}, s32[]{:T(128)}, s32[]{:T(128)}, bf16[512,1,128]{2,0,1:T(8,128)(2,1)S(1)}, /*index=5*/f32[8192,1]{0,1:T(1,128)}, ...), branch_computations={%region_21.21_spmd, %region_22.22_spmd} | conditional | flops 337970176 | bytes 7756894 | solution.py:37
  474.3 1.9 dynamic_update_slice.14
  477.4 7.9 %conditional.12 = ((f32[512,1,128]{0,2,1:T(8,128)S(1)}, f32[512,1,128]{0,2,1:T(8,128)S(1)}, f32[8192,1,128]{2,0,1:T(8,128)})) conditional(s32[]{:T(128)} %convert_element_type.146, (bf16[16,512,128]{2,1,0:T(8,128)(2,1)}, s32[]{:T(128)}, s32[]{:T(128)}, s32[]{:T(128)}, bf16[512,1,128]{2,0,1:T(8,128)(2,1)S(1)}, /*index=5*/f32[8192,1]{0,1:T(1,128)}, ...), branch_computations={%region_21.21_spmd, %region_22.22_spmd} | conditional | flops 337970176 | bytes 7756894 | solution.py:37
  483.5 1.9 dynamic_update_slice.14
  486.6 7.9 %conditional.12 = ((f32[512,1,128]{0,2,1:T(8,128)S(1)}, f32[512,1,128]{0,2,1:T(8,128)S(1)}, f32[8192,1,128]{2,0,1:T(8,128)})) conditional(s32[]{:T(128)} %convert_element_type.146, (bf16[16,512,128]{2,1,0:T(8,128)(2,1)}, s32[]{:T(128)}, s32[]{:T(128)}, s32[]{:T(128)}, bf16[512,1,128]{2,0,1:T(8,128)(2,1)S(1)}, /*index=5*/f32[8192,1]{0,1:T(1,128)}, ...), branch_computations={%region_21.21_spmd, %region_22.22_spmd} | conditional | flops 337970176 | bytes 7756894 | solution.py:37
  492.6 1.9 dynamic_update_slice.14
  495.7 7.9 %conditional.12 = ((f32[512,1,128]{0,2,1:T(8,128)S(1)}, f32[512,1,128]{0,2,1:T(8,128)S(1)}, f32[8192,1,128]{2,0,1:T(8,128)})) conditional(s32[]{:T(128)} %convert_element_type.146, (bf16[16,512,128]{2,1,0:T(8,128)(2,1)}, s32[]{:T(128)}, s32[]{:T(128)}, s32[]{:T(128)}, bf16[512,1,128]{2,0,1:T(8,128)(2,1)S(1)}, /*index=5*/f32[8192,1]{0,1:T(1,128)}, ...), branch_computations={%region_21.21_spmd, %region_22.22_spmd} | conditional | flops 337970176 | bytes 7756894 | solution.py:37
  501.7 1.9 dynamic_update_slice.14
  504.9 7.9 %conditional.12 = ((f32[512,1,128]{0,2,1:T(8,128)S(1)}, f32[512,1,128]{0,2,1:T(8,128)S(1)}, f32[8192,1,128]{2,0,1:T(8,128)})) conditional(s32[]{:T(128)} %convert_element_type.146, (bf16[16,512,128]{2,1,0:T(8,128)(2,1)}, s32[]{:T(128)}, s32[]{:T(128)}, s32[]{:T(128)}, bf16[512,1,128]{2,0,1:T(8,128)(2,1)S(1)}, /*index=5*/f32[8192,1]{0,1:T(1,128)}, ...), branch_computations={%region_21.21_spmd, %region_22.22_spmd} | conditional | flops 337970176 | bytes 7756894 | solution.py:37
  510.9 1.9 dynamic_update_slice.14
  514.0 7.9 %conditional.12 = ((f32[512,1,128]{0,2,1:T(8,128)S(1)}, f32[512,1,128]{0,2,1:T(8,128)S(1)}, f32[8192,1,128]{2,0,1:T(8,128)})) conditional(s32[]{:T(128)} %convert_element_type.146, (bf16[16,512,128]{2,1,0:T(8,128)(2,1)}, s32[]{:T(128)}, s32[]{:T(128)}, s32[]{:T(128)}, bf16[512,1,128]{2,0,1:T(8,128)(2,1)S(1)}, /*index=5*/f32[8192,1]{0,1:T(1,128)}, ...), branch_computations={%region_21.21_spmd, %region_22.22_spmd} | conditional | flops 337970176 | bytes 7756894 | solution.py:37
  523.1 7.9 %conditional.12 = ((f32[512,1,128]{0,2,1:T(8,128)S(1)}, f32[512,1,128]{0,2,1:T(8,128)S(1)}, f32[8192,1,128]{2,0,1:T(8,128)})) conditional(s32[]{:T(128)} %convert_element_type.146, (bf16[16,512,128]{2,1,0:T(8,128)(2,1)}, s32[]{:T(128)}, s32[]{:T(128)}, s32[]{:T(128)}, bf16[512,1,128]{2,0,1:T(8,128)(2,1)S(1)}, /*index=5*/f32[8192,1]{0,1:T(1,128)}, ...), branch_computations={%region_21.21_spmd, %region_22.22_spmd} | conditional | flops 337970176 | bytes 7756894 | solution.py:37
  532.3 7.8 %conditional.12 = ((f32[512,1,128]{0,2,1:T(8,128)S(1)}, f32[512,1,128]{0,2,1:T(8,128)S(1)}, f32[8192,1,128]{2,0,1:T(8,128)})) conditional(s32[]{:T(128)} %convert_element_type.146, (bf16[16,512,128]{2,1,0:T(8,128)(2,1)}, s32[]{:T(128)}, s32[]{:T(128)}, s32[]{:T(128)}, bf16[512,1,128]{2,0,1:T(8,128)(2,1)S(1)}, /*index=5*/f32[8192,1]{0,1:T(1,128)}, ...), branch_computations={%region_21.21_spmd, %region_22.22_spmd} | conditional | flops 337970176 | bytes 7756894 | solution.py:37
  540.0 3.8 convert_element_type.87
  548.5 10.9 %reduce-scatter.12.cloned.1.call-done = bf16[128,1,128]{2,0,1:T(8,128)(2,1)} async-done(((bf16[2048,1,128]{2,0,1:T(8,128)(2,1)}), bf16[128,1,128]{2,0,1:T(8,128)(2,1)}) %reduce-scatter.12.cloned.1.call-update) | async-done | bytes 32784 | tf_op jit(solution)/shard_map/reduce_scatter | solution.py:271
  560.8 78.1 %reduce-scatter.16.cloned.1.call-done = bf16[128,512]{1,0:T(8,128)(2,1)} async-done(((bf16[2048,512]{1,0:T(8,128)(2,1)}), bf16[128,512]{1,0:T(8,128)(2,1)}) %reduce-scatter.16.cloned.1.call-update) | async-done | bytes 131088
  642.2 72.7 %reduce-scatter.10.cloned.1.call-done = bf16[512,1,128]{2,0,1:T(8,128)(2,1)} async-done(((bf16[8192,1,128]{2,0,1:T(8,128)(2,1)}), bf16[512,1,128]{2,0,1:T(8,128)(2,1)}) %reduce-scatter.10.cloned.1.call-update) | async-done | bytes 131088 | tf_op jit(solution)/shard_map/reduce_scatter | solution.py:219
  (482 shorter events, 210.6 us)
Async XLA Ops:
  7.2 57.2 %copy-start = (bf16[128,2048]{1,0:T(8,128)(2,1)S(1)}, bf16[128,2048]{1,0:T(8,128)(2,1)}, u32[]{:S(2)}) copy-start(bf16[128,2048]{1,0:T(8,128)(2,1)} %param.34) | copy-start | bytes 1572868
  7.2 60.9 %copy-start.14 = (bf16[128,128]{1,0:T(8,128)(2,1)S(1)}, bf16[128,128]{1,0:T(8,128)(2,1)}, u32[]{:S(2)}) copy-start(bf16[128,128]{1,0:T(8,128)(2,1)} %param.31) | copy-start | bytes 98308
  7.2 97.5 %copy-start.9 = (s32[512,4]{0,1:T(4,128)S(1)}, s32[512,4]{0,1:T(4,128)}, u32[]{:S(2)}) copy-start(s32[512,4]{0,1:T(4,128)} %param.33) | copy-start | bytes 24580
  7.2 97.5 %copy-start.1 = (bf16[512,128]{1,0:T(8,128)(2,1)S(1)}, bf16[512,128]{1,0:T(8,128)(2,1)}, u32[]{:S(2)}) copy-start(bf16[512,128]{1,0:T(8,128)(2,1)} %param.30) | copy-start | bytes 393220
  7.2 57.1 %all-gather.14.cloned.1.call-start = ((), (), s32[]{:S(2)}) async-start(), calls=%async_computation.8 | async-start | bytes 2228224 | tf_op jit(solution)/shard_map/all_gather | solution.py:148
  7.9 155.5 %all-gather.10.cloned.1.call-start = ((), (), s32[]{:S(2)}) async-start(), calls=%async_computation.6 | async-start | bytes 2228224 | tf_op jit(solution)/shard_map/all_gather | solution.py:127
  8.7 200.8 %all-gather.8.cloned.1.call-start = ((), (), s32[]{:S(2)}) async-start(), calls=%async_computation.5 | async-start | bytes 2228224 | tf_op jit(solution)/shard_map/all_gather | solution.py:128
  9.4 379.0 %all-gather.16.cloned.1.call-start = ((), (), s32[]{:S(2)}) async-start(), calls=%async_computation.9 | async-start | bytes 2228224 | tf_op jit(solution)/shard_map/all_gather | solution.py:214
  67.5 324.2 %all-gather.12.cloned.1.call-start = ((), (), s32[]{:S(2)}) async-start(), calls=%async_computation.7 | async-start | bytes 2228224 | tf_op jit(solution)/shard_map/all_gather | solution.py:213
  68.0 477.5 %reduce-scatter.18.cloned.1.call-start = ((), (), s32[]{:S(2)}) async-start(), calls=%async_computation.14 | async-start | bytes 557056
  104.7 11.8 %copy-start.15 = (bf16[128,128]{1,0:T(8,128)(2,1)S(1)}, bf16[128,128]{1,0:T(8,128)(2,1)}, u32[]{:S(2)}) copy-start(bf16[128,128]{1,0:T(8,128)(2,1)} %param.32) | copy-start | bytes 98308
  151.4 12.0 %copy-start.8 = (bf16[512,128]{0,1:T(8,128)(2,1)S(1)}, bf16[512,128]{0,1:T(8,128)(2,1)}, u32[]{:S(2)}) copy-start(bf16[512,128]{0,1:T(8,128)(2,1)} %convolution_convert_fusion.2) | copy-start | bytes 393220
  151.4 12.2 %copy-start.13 = (bf16[512,128]{1,0:T(8,128)(2,1)S(1)}, bf16[512,128]{1,0:T(8,128)(2,1)}, u32[]{:S(2)}) copy-start(bf16[512,128]{1,0:T(8,128)(2,1)} %param.27) | copy-start | bytes 393220
  163.3 0.8 copy-start.7
  163.3 0.9 copy-start.12
  210.7 35.8 %copy-start.5 = (bf16[512,2048]{1,0:T(8,128)(2,1)S(1)}, bf16[512,2048]{1,0:T(8,128)(2,1)}, u32[]{:S(2)}) copy-start(bf16[512,2048]{1,0:T(8,128)(2,1)} %all-gather.14.cloned.1.call-done) | copy-start | bytes 6291460
  245.8 0.7 copy-start.10
  249.8 297.3 %reduce-scatter.14.cloned.1.call-start = ((), (), s32[]{:S(2)}) async-start(), calls=%async_computation.12 | async-start | bytes 557056 | tf_op jit(solution)/shard_map/reduce_scatter | solution.py:274
  252.8 1.6 copy-start.2
  254.7 0.7 copy-start.3
  258.2 1.6 copy-start.2
  260.0 0.7 copy-start.3
  263.5 1.6 copy-start.2
  265.4 0.7 copy-start.3
  268.8 1.6 copy-start.2
  270.7 0.7 copy-start.3
  271.4 1.9 copy-start.11
  272.3 287.1 %reduce-scatter.12.cloned.1.call-start = ((), (), s32[]{:S(2)}) async-start(), calls=%async_computation.11 | async-start | bytes 557056 | tf_op jit(solution)/shard_map/reduce_scatter | solution.py:271
  273.2 365.7 %reduce-scatter.16.cloned.1.call-start = ((), (), s32[]{:S(2)}) async-start(), calls=%async_computation.13 | async-start | bytes 2228224
  276.6 0.7 copy-start.17
  276.6 80.2 %copy-start.16 = (f32[512]{0:T(512)S(1)}, f32[512]{0:T(512)}, u32[]{:S(2)}) copy-start(f32[512]{0:T(512)} %get-tuple-element.1271) | copy-start | bytes 6148
  276.6 438.3 %reduce-scatter.10.cloned.1.call-start = ((), (), s32[]{:S(2)}) async-start(), calls=%async_computation.10 | async-start | bytes 2228224 | tf_op jit(solution)/shard_map/reduce_scatter | solution.py:219
  391.7 2.2 copy-start.6
  543.8 1.0 copy-start.4
Sparse Core Ops, SparseCore 0:
  10.7 53.6 all-gather.13
  66.1 71.7 all-gather.9
  139.8 69.6 all-gather.7
  211.7 69.0 all-gather.15
  282.4 68.8 all-gather.11
  353.7 67.3 reduce-scatter.17
  423.8 66.6 reduce-scatter.13
  492.9 66.4 reduce-scatter.11
  564.2 74.6 reduce-scatter.15
  641.3 73.6 reduce-scatter.9
where the time goes:
time: 727 us; the launch traced here: 723 us
  waiting for transfers between devices  241 us (33%)
  blocking collectives  183 us (25%)
  local copies, waits for them, and re-layouts  112 us (15%)
  matrix products  106 us (15%)
  loops' own time  43.1 us (6%)
  other arithmetic  23.4 us (3%)
  between operations  14.5 us (2%)
    unnamed x12, waiting for transfers between devices  80.8 us
    all_gather x1, blocking collectives, shards(): lax.all_gather(self_lse, 'ctx', axis=0, tiled=True)  79.5 us
    reduce_scatter x1, waiting for transfers between devices, shards(): lax.psum_scatter(result[2].astype(jnp.bfloat16), 'ctx', scatter_dimension...  72.7 us
    all_gather x1, waiting for transfers between devices, shards(): full_cotangent = lax.all_gather(cotangent, 'row', axis=1, tiled=True)  54.9 us
    dynamic_slice x60, local copies, waits for them, and re-layouts, in_blocks(): lax.scan(advance, state, (jnp.arange(block_count, dtype=jnp.int32), stack...  44.8 us
    another operation x6, loops' own time, in_blocks(): lax.scan(advance, state, (jnp.arange(block_count, dtype=jnp.int32), stack...  41.4 us
    all_gather x1, blocking collectives, shards(): lax.all_gather(row_keys, 'ctx', axis=0, tiled=True)  36.6 us
    all_gather x1, blocking collectives, shards(): lax.all_gather(row_values, 'ctx', axis=0, tiled=True)  34.9 us
  transfers between devices with their start and end apart: 10, of which 5 were waited for; matrix products, arithmetic and copies ran while one was open for 33% of the time, Pallas kernels for 0%

commit v1 on v0

v1 whole, which is shorter than its diff:
```python
import functools
import math

import jax
import jax.numpy as jnp
from jax import lax
from jax.experimental import pallas as pl
from jax.experimental.pallas import tpu as pltpu
from jax.sharding import PartitionSpec as P

MESH = pl.DeviceIdType.MESH
F32 = jnp.float32
BF16 = jnp.bfloat16
T = 512
HD = 128
TR = 128
NC = 16
NZ = 8
SCALE = 1.0 / math.sqrt(HD)
C2 = SCALE * math.log2(math.e)
LOG2E = math.log2(math.e)
NEG = -1e30

K0, RK0, V0, RV0, AG_HALF, AG_ALL = 0, 512, 640, 1152, 640, 1280
DK0, DRK0, GT0, DV0, DRV0, GB0, RS_HALF, RS_ALL = 0, 512, 640, 704, 1216, 1344, 704, 1408


def nn(a, b):
    return lax.dot_general(a, b, (((1,), (0,)), ((), ())), preferred_element_type=F32)


def nt(a, b):
    return lax.dot_general(a, b, (((1,), (1,)), ((), ())), preferred_element_type=F32)


def tn(a, b):
    return lax.dot_general(a, b, (((0,), (0,)), ((), ())), preferred_element_type=F32)


def body(
    q_ref, cq_ref, inc_ref, w_ref, k_hbm, v_hbm, rk_hbm, rv_hbm, cot_hbm,
    mixed_ref, gq_ref, gk_ref, gv_ref, gcq_ref, grk_ref, grv_ref, gw_ref,
    kv, cot, hid, wcol, snd, rcv, part, xsnd, xrcv, qt, cqt, dot_t, do_ref, ht,
    acc_s, acc_c, m_s, l_s, m_c, l_c, dl_s, dl_c, bias, dq_t, dcq_t,
    lsem, agx_s, agx_r, agz_s, agz_r, rsz_s, rsz_r, rsx_s, rsx_r, row_s, row_r, w_s, w_r,
):
    c = lax.axis_index("ctx")
    r = lax.axis_index("row")
    p, z = c // NZ, c % NZ
    y, xh, core = r // 4, (r // 2) % 2, r % 2

    def ctx_at(plane, depth):
        return {"ctx": plane * NZ + (depth + NZ) % NZ}

    def row_at(yy, xx, cc):
        return {"row": (((yy + 4) % 4) * 2 + xx) * 2 + cc}

    def plane_of(j):
        return p + j * (1 - 2 * p)

    def zmod(d):
        return (z + d + NZ) % NZ

    def remote(src, dst, ssem, rsem, device):
        return pltpu.make_async_remote_copy(
            src_ref=src, dst_ref=dst, send_sem=ssem, recv_sem=rsem, device_id=device, device_id_type=MESH
        )

    def agx():
        return remote(kv.at[p, z], kv.at[p, z], agx_s.at[0], agx_r.at[0], ctx_at(1 - p, z))

    def agx_in():
        return remote(kv.at[1 - p, z], kv.at[1 - p, z], agx_s.at[0], agx_r.at[0], ctx_at(1 - p, z))

    def agz(s, way, j, origin, half):
        ref = kv.at[plane_of(j), origin]
        if half:
            ref = ref.at[pl.ds(way * AG_HALF, AG_HALF)]
        return remote(ref, ref, agz_s.at[s - 1, way, j], agz_r.at[s - 1, way, j], ctx_at(p, z + 1 - 2 * way))

    def agz_out(s, way, j, half=False):
        return agz(s, way, j, zmod((2 * way - 1) * (s - 1)), half)

    def agz_in(s, way, j, half=False):
        return agz(s, way, j, zmod((2 * way - 1) * s), half)

    def rsz(s, way, j, half=False):
        src, dst = snd.at[s - 1, way, j], rcv.at[s - 1, way, j]
        if half:
            src = snd.at[0, 0, j].at[pl.ds(way * RS_HALF, RS_HALF)]
            dst = dst.at[pl.ds(way * RS_HALF, RS_HALF)]
        return remote(src, dst, rsz_s.at[s - 1, way, j], rsz_r.at[s - 1, way, j], ctx_at(p, z + 1 - 2 * way))

    def rsx():
        return remote(xsnd, xrcv, rsx_s.at[0], rsx_r.at[0], ctx_at(1 - p, z))

    def row_copy(buf, k, n, out):
        up, down, sib = row_at(y + 1, xh, core), row_at(y - 1, xh, core), row_at(y, xh, 1 - core)
        ym, yp, y2 = (y + 3) % 4, (y + 1) % 4, (y + 2) % 4
        mine, other = (core, core) if n < 5 else (core, 1 - core)
        if n == 0:
            ref = buf.at[y, core, xh if out else 1 - xh]
            dev = row_at(y, 1 - xh, core)
        elif n == 1:
            ref, dev = buf.at[y if out else ym, core], up
        elif n == 2:
            ref, dev = buf.at[y if out else yp, core], down
        elif n == 3:
            ref, dev = buf.at[ym if out else y2, core, :, pl.ds(0, T // 2)], up
        elif n == 4:
            ref, dev = buf.at[yp if out else y2, core, :, pl.ds(T // 2, T // 2)], down
        else:
            at = (y, ym, yp, y2)[n - 5]
            ref, dev = buf.at[at, mine if out else other], sib
        return remote(ref, ref, row_s.at[k, n], row_r.at[k, n], dev)

    def row_stage(buf, k, stage):
        waits, starts = {
            0: ((), (0,)), 1: ((0,), (1, 2, 5)), 2: ((1, 2), (3, 4, 6, 7)), 3: ((3, 4), (8,)), 4: ((5, 6, 7, 8), ()),
        }[stage]
        for n in waits:
            row_copy(buf, k, n, False).wait_recv()
        for n in starts:
            row_copy(buf, k, n, True).start()

    def w_out(j):
        to = (r + j) % NC
        return remote(
            w_ref.at[:, pl.ds(pl.multiple_of(to * HD, HD), HD)], wcol.at[r], w_s.at[j], w_r.at[j], {"row": to}
        )

    def w_in(j):
        at = (r + NC - j) % NC
        return remote(wcol.at[at], wcol.at[at], w_s.at[j], w_r.at[j], {"row": at})

    own = kv.at[p, z]
    loads = [
        pltpu.make_async_copy(k_hbm, own.at[pl.ds(K0, T)], lsem.at[0]),
        pltpu.make_async_copy(rk_hbm, own.at[pl.ds(RK0, TR)], lsem.at[1]),
        pltpu.make_async_copy(v_hbm, own.at[pl.ds(V0, T)], lsem.at[2]),
        pltpu.make_async_copy(rv_hbm, own.at[pl.ds(RV0, TR)], lsem.at[3]),
        pltpu.make_async_copy(cot_hbm, cot.at[y, core, xh], lsem.at[4]),
        pltpu.make_async_copy(w_ref.at[:, pl.ds(pl.multiple_of(r * HD, HD), HD)], wcol.at[r], lsem.at[5]),
    ]
    for load in loads:
        load.start()
    barrier = pltpu.get_barrier_semaphore()
    for device in (ctx_at(1 - p, z), ctx_at(p, z + 1), ctx_at(p, z - 1)):
        pl.semaphore_signal(barrier, inc=1, device_id=device, device_id_type=MESH)

    def greet(j, carry):
        pl.semaphore_signal(barrier, inc=1, device_id={"row": (r + j) % NC}, device_id_type=MESH)
        return carry

    lax.fori_loop(1, NC, greet, 0)
    for load in loads:
        load.wait()
    pl.semaphore_wait(barrier, NC + 2)

    agx().start()
    agz_out(1, 0, 0).start()
    agz_out(1, 1, 0).start()
    row_stage(cot, 0, 0)

    qt[...] = jnp.transpose(q_ref[...].astype(F32)).astype(BF16)
    cqt[...] = jnp.transpose(cq_ref[...].astype(F32)).astype(BF16)
    lanes = lax.broadcasted_iota(jnp.int32, (T, HD), 1)
    hit = jnp.zeros((T, HD), F32)
    for n in range(4):
        hit = jnp.where(inc_ref[:, n : n + 1] == lanes, 1.0, hit)
    bias[...] = (jnp.transpose(hit)[0:NC, :] - 1.0) * (-NEG)
    for ref in (acc_s, acc_c, l_s, l_c, dq_t, dcq_t):
        ref[...] = jnp.zeros_like(ref)
    for ref in (m_s, m_c):
        ref[...] = jnp.full_like(ref, NEG)
    for j in range(2):
        rcv[0, 0, j, RS_HALF:, :] = jnp.zeros((RS_ALL - RS_HALF, HD), BF16)
        rcv[0, 1, j, :RS_HALF, :] = jnp.zeros((RS_HALF, HD), BF16)

    def online(logits, values, m_ref, l_ref, acc_ref):
        m_old = m_ref[...]
        m_new = jnp.maximum(m_old, jnp.max(logits, axis=0, keepdims=True))
        probs = jnp.exp2(logits - m_new)
        fade = jnp.exp2(m_old - m_new)
        l_ref[...] = l_ref[...] * fade + jnp.sum(probs, axis=0, keepdims=True)
        acc_ref[...] = acc_ref[...] * fade + tn(values, probs.astype(BF16))
        m_ref[...] = m_new

    def causal(x, fill):
        keep = lax.broadcasted_iota(jnp.int32, (T, T), 0) <= lax.broadcasted_iota(jnp.int32, (T, T), 1)
        return jnp.where(keep, x, fill)

    def self_forward(pa, zb, diagonal):
        logits = nn(kv[pa, zb, pl.ds(K0, T), :], qt[...]) * C2
        if diagonal:
            logits = causal(logits, NEG)
        online(logits, kv[pa, zb, pl.ds(V0, T), :], m_s, l_s, acc_s)

    def cross_logits(pa, zb):
        return nn(kv[pa, zb, pl.ds(RK0, TR), :], cqt[...]) * C2 + bias[pl.ds(pa * NZ + zb, 1), :]

    def cross_forward(pa, zb):
        online(cross_logits(pa, zb), kv[pa, zb, pl.ds(RV0, TR), :], m_c, l_c, acc_c)

    self_forward(p, z, True)
    cross_forward(p, z)

    def forward_step(t, carry):
        v = t - 2
        s = jnp.where(t < 2, 0, v // 4 + 1)
        i = jnp.where(t < 2, 1, v % 4)
        way, j = i // 2, i % 2

        @pl.when(t == 1)
        def _():
            agx_in().wait_recv()
            agz_out(1, 0, 1).start()
            agz_out(1, 1, 1).start()
            row_stage(cot, 0, 1)

        for hop in range(1, 5):

            @pl.when(v == 4 * (hop - 1))
            def _():
                for jj in range(2):
                    for ww in range(2):
                        agz_in(hop, ww, jj, hop == 4).wait_recv()
                        if hop < 4:
                            agz_out(hop + 1, ww, jj, hop == 3).start()
                if hop == 1:
                    for jj in range(1, NC):
                        w_out(jj).start()
                if hop > 1:
                    row_stage(cot, 0, hop)

        pa = plane_of(j)
        zb = zmod((2 * way - 1) * s)

        @pl.when(pa * NZ + zb < c)
        def _():
            self_forward(pa, zb, False)

        cross_forward(pa, zb)
        return carry

    lax.fori_loop(1, NC, forward_step, 0)

    grad = jnp.zeros((T, HD), F32)
    for n in range(NC):
        grad = grad + nt(cot[n // 4, n % 2, (n // 2) % 2], w_ref[:, n * HD : (n + 1) * HD])
    grad = grad.astype(BF16)
    do_ref[...] = grad
    grad_t = jnp.transpose(grad.astype(F32))
    dot_t[...] = grad_t.astype(BF16)
    out_s = acc_s[...] / l_s[...]
    out_c = acc_c[...] / l_c[...]
    hidden_t = out_s + out_c
    ht[...] = hidden_t.astype(BF16)
    hid[y, core, xh] = jnp.transpose(hidden_t).astype(BF16)
    dl_s[...] = jnp.sum(grad_t * out_s, axis=0, keepdims=True)
    dl_c[...] = jnp.sum(grad_t * out_c, axis=0, keepdims=True)
    m_s[...] = m_s[...] + jnp.log(l_s[...]) * LOG2E
    m_c[...] = m_c[...] + jnp.log(l_c[...]) * LOG2E
    row_stage(hid, 1, 0)

    def logit_grads(logits, lse_ref, delta_ref, values, diagonal):
        probs = jnp.exp2(logits - lse_ref[...])
        if diagonal:
            probs = causal(probs, 0.0)
        dlogits = probs * (nn(values, dot_t[...]) - delta_ref[...])
        return probs.astype(BF16), dlogits.astype(BF16)

    def self_backward(pa, zb, slot, diagonal):
        keys, values = kv[pa, zb, pl.ds(K0, T), :], kv[pa, zb, pl.ds(V0, T), :]
        probs, dlogits = logit_grads(nn(keys, qt[...]) * C2, m_s, dl_s, values, diagonal)
        part[slot, pl.ds(DV0, T), :] = nn(probs, do_ref[...])
        part[slot, pl.ds(DK0, T), :] = nn(dlogits, q_ref[...])
        dq_t[...] += tn(keys, dlogits)

    def cross_backward(pa, zb, slot):
        probs, dlogits = logit_grads(cross_logits(pa, zb), m_c, dl_c, kv[pa, zb, pl.ds(RV0, TR), :], False)
        part[slot, pl.ds(DRV0, TR), :] = nn(probs, do_ref[...])
        part[slot, pl.ds(DRK0, TR), :] = nn(dlogits, cq_ref[...])
        dcq_t[...] += tn(kv[pa, zb, pl.ds(RK0, TR), :], dlogits)
        b = pa * NZ + zb
        weight = nn(ht[...], cot[b // 4, b % 2, (b // 2) % 2])
        part[slot, pl.ds(GT0, HD // 2), :] = weight[: HD // 2]
        part[slot, pl.ds(GB0, HD // 2), :] = weight[HD // 2 :]

    def backward_step(u, carry):
        v = u - 2
        first, last = u < 2, u == 14
        s = jnp.where(first, 1, v // 4 + 2)
        i = jnp.where(first, u, jnp.where(last, 1, v % 4))
        way, j = i // 2, i % 2
        slot = jnp.where(first, u, v % 4)
        d = 5 - s
        pa = plane_of(j)
        zb = zmod((1 - 2 * way) * d)

        @pl.when(pa * NZ + zb < c)
        def _():
            self_backward(pa, zb, slot, False)

        @pl.when(pa * NZ + zb > c)
        def _():
            part[slot, pl.ds(DK0, T), :] = jnp.zeros((T, HD), F32)
            part[slot, pl.ds(DV0, T), :] = jnp.zeros((T, HD), F32)

        cross_backward(pa, zb, slot)

        @pl.when(u == 1)
        def _():
            for jj in range(2):
                snd[0, 0, jj] = part[jj].astype(BF16)
                rsz(1, 0, jj, True).start()
                rsz(1, 1, jj, True).start()
            row_stage(hid, 1, 1)

        for hop in range(2, 5):

            @pl.when(v == 4 * (hop - 2) + 3)
            def _():
                def pass_on(n, inner):
                    ww, jj = n // 2, n % 2
                    rsz(hop - 1, ww, jj, hop == 2).wait_recv()
                    snd[hop - 1, ww, jj] = (part[n] + rcv[hop - 2, ww, jj].astype(F32)).astype(BF16)
                    rsz(hop, ww, jj).start()
                    return inner

                lax.fori_loop(0, 4, pass_on, 0)
                row_stage(hid, 1, hop)

        return carry

    lax.fori_loop(0, NC - 1, backward_step, 0)
    self_backward(p, z, 1, True)
    cross_backward(p, z, 1)

    for j in range(1, NC):
        w_in(j).wait_recv()
    mix = jnp.zeros((T, HD), F32)
    for n in range(NC):
        mix = mix + nn(hid[n // 4, n % 2, (n // 2) % 2], wcol[n])
    mixed_ref[...] = mix.astype(BF16)
    gq_ref[...] = jnp.transpose(dq_t[...]) * SCALE
    gcq_ref[...] = jnp.transpose(dcq_t[...]) * SCALE

    rsz(4, 0, 1).wait_recv()
    rsz(4, 1, 1).wait_recv()
    xsnd[...] = (part[0] + rcv[3, 0, 1].astype(F32) + rcv[3, 1, 1].astype(F32)).astype(BF16)
    rsx().start()
    rsz(4, 0, 0).wait_recv()
    rsz(4, 1, 0).wait_recv()
    part[1] = part[1] + rcv[3, 0, 0].astype(F32) + rcv[3, 1, 0].astype(F32)
    rsx().wait_recv()

    def total(at, rows):
        return part[1, pl.ds(at, rows), :] + xrcv[pl.ds(at, rows), :].astype(F32)

    gk_ref[...] = total(DK0, T) * SCALE
    gv_ref[...] = total(DV0, T)
    grk_ref[...] = total(DRK0, TR) * SCALE
    grv_ref[...] = total(DRV0, TR)
    gw_ref[pl.ds(0, HD // 2), :] = total(GT0, HD // 2)
    gw_ref[pl.ds(HD // 2, HD // 2), :] = total(GB0, HD // 2)

    agx().wait_send()
    rsx().wait_send()
    for jj in range(2):
        for ww in range(2):
            for s in range(1, 5):
                agz_out(s, ww, jj, s == 4).wait_send()
                rsz(s, ww, jj, s == 1).wait_send()
    for n in range(9):
        row_copy(cot, 0, n, True).wait_send()
        row_copy(hid, 1, n, True).wait_send()
    for j in range(1, NC):
        w_out(j).wait_send()


def shards(queries, keys, values, cross_queries, row_keys, row_values, incidence, out_weight, cotangent):
    vmem = pl.BlockSpec(memory_space=pltpu.VMEM)
    hbm = pl.BlockSpec(memory_space=pl.ANY)
    dma = pltpu.SemaphoreType.DMA
    big, small = jax.ShapeDtypeStruct((T, HD), F32), jax.ShapeDtypeStruct((TR, HD), F32)
    wide = pltpu.VMEM((HD, T), F32)
    line = pltpu.VMEM((1, T), F32)
    return pl.pallas_call(
        body,
        out_shape=(jax.ShapeDtypeStruct((T, HD), BF16), big, big, big, big, small, small, small),
        in_specs=[vmem] * 4 + [hbm] * 5,
        out_specs=[vmem] * 8,
        scratch_shapes=[
            pltpu.VMEM((2, NZ, AG_ALL, HD), BF16),
            pltpu.VMEM((4, 2, 2, T, HD), BF16),
            pltpu.VMEM((4, 2, 2, T, HD), BF16),
            pltpu.VMEM((NC, HD, HD), BF16),
            pltpu.VMEM((4, 2, 2, RS_ALL, HD), BF16),
            pltpu.VMEM((4, 2, 2, RS_ALL, HD), BF16),
            pltpu.VMEM((4, RS_ALL, HD), F32),
            pltpu.VMEM((RS_ALL, HD), BF16),
            pltpu.VMEM((RS_ALL, HD), BF16),
            pltpu.VMEM((HD, T), BF16),
            pltpu.VMEM((HD, T), BF16),
            pltpu.VMEM((HD, T), BF16),
            pltpu.VMEM((T, HD), BF16),
            pltpu.VMEM((HD, T), BF16),
            wide, wide, line, line, line, line, line, line,
            pltpu.VMEM((NC, T), F32),
            wide, wide,
            dma((6,)), dma((1,)), dma((1,)), dma((4, 2, 2)), dma((4, 2, 2)), dma((4, 2, 2)), dma((4, 2, 2)),
            dma((1,)), dma((1,)), dma((2, 9)), dma((2, 9)), dma((NC,)), dma((NC,)),
        ],
        compiler_params=pltpu.CompilerParams(
            collective_id=0, has_side_effects=True, vmem_limit_bytes=60 * 1024 * 1024
        ),
        name="attention_layer",
    )(queries, cross_queries, incidence, out_weight, keys, values, row_keys, row_values, cotangent)


def solution(mesh):
    both = P("ctx", "row")
    return jax.shard_map(
        shards,
        mesh=mesh,
        in_specs=(both, both, both, both, both, both, P("ctx", None), P("row", None), both),
        out_specs=(both, both, both, both, both, both, both, P("row", "ctx")),
        check_vma=False,
    )
```

time: 727 us -> 144 us (0.20)
  waiting for transfers between devices: 241 us -> 0 us
  blocking collectives: 183 us -> 0 us
  Pallas kernels: 0 us -> 134 us
  matrix products: 106 us -> 0 us
  local copies, waits for them, and re-layouts: 112 us -> 9.51 us
  loops' own time: 43.1 us -> 0 us
  other arithmetic: 23.4 us -> 0 us
  between operations: 14.5 us -> 0.66 us
    all_gather x4 -> x0, blocking collectives: 183 us -> none  [the longest x1 79.5 us: shards(): lax.all_gather(self_lse, 'ctx', axis=0, tiled=True)]
    pallas_call x0 -> x1, Pallas kernels: none -> 134 us  [shards(): pl.pallas_call(body, out_shape=(jax.ShapeDtypeStruct((T, HD), BF16), big,...]
    dot_general x113 -> x0, matrix products: 106 us -> none  [the longest x25 24.8 us: logits_of(): jnp.einsum('qhd,khd->qhk', queries_in, keys_in, preferred_element_type=jn...]
    reduce_scatter x3 -> x0, waiting for transfers between devices: 83.7 us -> none  [the longest x1 72.7 us: shards(): lax.psum_scatter(result[2].astype(jnp.bfloat16), 'ctx', scatter_dimension...]
    unnamed x12 -> x0, waiting for transfers between devices: 80.8 us -> none
    all_gather x5 -> x0, waiting for transfers between devices: 77 us -> none  [the longest x1 54.9 us: shards(): full_cotangent = lax.all_gather(cotangent, 'row', axis=1, tiled=True)]
    dynamic_slice x76 -> x0, local copies, waits for them, and re-layouts: 57 us -> none  [the longest x60 44.8 us: in_blocks(): lax.scan(advance, state, (jnp.arange(block_count, dtype=jnp.int32), stack...]
    another operation x54 -> x0, loops' own time: 43.1 us -> none  [the longest x6 41.4 us: in_blocks(): lax.scan(advance, state, (jnp.arange(block_count, dtype=jnp.int32), stack...]
  transfers between devices with their start and end apart: 10 -> 0, of which waited for: 5 -> 0; matrix products, arithmetic and copies ran while one was open for 33% -> 0% of each run, Pallas kernels for 0% -> 0%
where the time goes in v1:
time: 144 us
  Pallas kernels  134 us (93%)
  local copies, waits for them, and re-layouts  9.51 us (7%)
    pallas_call x1, Pallas kernels, shards(): pl.pallas_call(body, out_shape=(jax.ShapeDtypeStruct((T, HD), BF16), big,...  134 us
    unnamed x23, local copies, waits for them, and re-layouts  9.51 us

profile of v1, /device:TPU:8, one launch (start us, length us, event | category | flops | bytes accessed | tf_op | source)
XLA Modules:
  0.0 143.8 jit_solution(16341112350913321763)
XLA Ops:
  0.6 1.6 %copy.17.inc_ref = s32[512,4]{1,0:T(8,128)} copy(s32[512,4]{0,1:T(4,128)} %param.15) | data formatting | bytes 16384 | tf_op args[6]
  2.2 133.6 %attention_layer.1 = (bf16[512,128]{1,0:T(8,128)(2,1)}, f32[512,128]{1,0:T(8,128)}, f32[512,128]{1,0:T(8,128)}, f32[512,128]{1,0:T(8,128)}, f32[512,128]{1,0:T(8...) custom-call(bf16[512,128]{1,0:T(8,128)(2,1)} %q_ref.1, bf16[512,128]{1,0:T(8,128)(2,1)} %cq_ref.1, ...), custom_call_target="tpu_custom_call" | custom-call | tf_op jit(solution)/shard_map/attention_layer/pallas_call | solution.py:389
  135.8 0.0 copy-start.3
  135.8 1.6 %copy.26 = bf16[512,128]{1,0:T(8,128)(2,1)} copy(bf16[512,128]{1,0:T(8,128)(2,1)} %get-tuple-element.16) | data formatting | bytes 262144
  137.4 0.0 copy-done.3
  137.4 0.0 copy-start.2
  137.4 0.7 copy.27
  138.1 0.3 copy-done.2
  138.4 0.0 copy-start.1
  138.4 0.7 copy.28
  139.1 0.3 copy-done.1
  139.5 0.0 copy-start
  139.5 0.7 copy.29
  140.2 0.3 copy-done
  140.5 0.0 copy-start.6
  140.5 0.7 copy.30
  141.2 0.2 copy-done.6
  141.4 0.0 copy-start.5
  141.4 0.6 copy.31
  142.0 0.2 copy-done.5
  142.3 0.0 copy-start.4
  142.3 0.6 copy.32
  142.9 0.2 copy-done.4
  143.1 0.6 copy.33
Async XLA Ops:
  135.8 1.6 %copy-start.3 = (f32[512,128]{1,0:T(8,128)S(1)}, f32[512,128]{1,0:T(8,128)}, u32[]{:S(2)}) copy-start(f32[512,128]{1,0:T(8,128)} %get-tuple-element.17) | copy-start | bytes 786436
  137.4 1.0 copy-start.2
  138.4 1.0 copy-start.1
  139.5 1.0 copy-start
  140.5 0.9 copy-start.6
  141.4 0.9 copy-start.5
  142.3 0.9 copy-start.4

commit v2 on v1

--- a/solution.py
+++ b/solution.py
@@ -21,8 +21,10 @@
 LOG2E = math.log2(math.e)
 NEG = -1e30
 
-K0, RK0, V0, RV0, AG_HALF, AG_ALL = 0, 512, 640, 1152, 640, 1280
-DK0, DRK0, GT0, DV0, DRV0, GB0, RS_HALF, RS_ALL = 0, 512, 640, 704, 1216, 1344, 704, 1408
+K0, RK0, RV0, V0, AG_HALF, AG_ALL = 0, 512, 640, 768, 640, 1280
+AG_MID, AG_MID_N = 512, 256
+DK0, DRK0, GT0, GB0, DRV0, DV0, RS_HALF, RS_ALL = 0, 512, 640, 704, 768, 896, 704, 1408
+RS_MID, RS_MID_N = 512, 384
 
 
 def nn(a, b):
@@ -41,8 +43,9 @@
     q_ref, cq_ref, inc_ref, w_ref, k_hbm, v_hbm, rk_hbm, rv_hbm, cot_hbm,
     mixed_ref, gq_ref, gk_ref, gv_ref, gcq_ref, grk_ref, grv_ref, gw_ref,
     kv, cot, hid, wcol, snd, rcv, part, xsnd, xrcv, qt, cqt, dot_t, do_ref, ht,
-    acc_s, acc_c, m_s, l_s, m_c, l_c, dl_s, dl_c, bias, dq_t, dcq_t,
+    acc_s, acc_c, m_s, l_s, m_c, l_c, dl_s, dl_c, bias, dq_t, dcq_t, xr,
     lsem, agx_s, agx_r, agz_s, agz_r, rsz_s, rsz_r, rsx_s, rsx_r, row_s, row_r, w_s, w_r,
+    rel_s, rel_r, shr_s, shr_r,
 ):
     c = lax.axis_index("ctx")
     r = lax.axis_index("row")
@@ -66,33 +69,105 @@
             src_ref=src, dst_ref=dst, send_sem=ssem, recv_sem=rsem, device_id=device, device_id_type=MESH
         )
 
-    def agx():
-        return remote(kv.at[p, z], kv.at[p, z], agx_s.at[0], agx_r.at[0], ctx_at(1 - p, z))
-
-    def agx_in():
-        return remote(kv.at[1 - p, z], kv.at[1 - p, z], agx_s.at[0], agx_r.at[0], ctx_at(1 - p, z))
-
-    def agz(s, way, j, origin, half):
-        ref = kv.at[plane_of(j), origin]
-        if half:
+    def on_plane(plane, act):
+        pl.when(p == plane)(act)
+
+    def agx(out, plane):
+        ref = kv.at[p if out else 1 - p, z]
+        if (plane == 1) == out:
+            ref = ref.at[pl.ds(AG_MID, AG_MID_N)]
+        return remote(ref, ref, agx_s.at[0], agx_r.at[0], ctx_at(1 - p, z))
+
+    def agz(s, way, j, out, middle):
+        ref = kv.at[plane_of(j), zmod((2 * way - 1) * (s - 1 if out else s))]
+        half = s == 4
+        if middle:
+            n = AG_MID_N // 2 if half else AG_MID_N
+            ref = ref.at[pl.ds(AG_MID + (way * n if half else 0), n)]
+        elif half:
             ref = ref.at[pl.ds(way * AG_HALF, AG_HALF)]
         return remote(ref, ref, agz_s.at[s - 1, way, j], agz_r.at[s - 1, way, j], ctx_at(p, z + 1 - 2 * way))
 
-    def agz_out(s, way, j, half=False):
-        return agz(s, way, j, zmod((2 * way - 1) * (s - 1)), half)
-
-    def agz_in(s, way, j, half=False):
-        return agz(s, way, j, zmod((2 * way - 1) * s), half)
-
-    def rsz(s, way, j, half=False):
-        src, dst = snd.at[s - 1, way, j], rcv.at[s - 1, way, j]
-        if half:
-            src = snd.at[0, 0, j].at[pl.ds(way * RS_HALF, RS_HALF)]
-            dst = dst.at[pl.ds(way * RS_HALF, RS_HALF)]
+    def relay(s, way):
+        ref = kv.at[0, zmod((2 * way - 1) * s)]
+        if s == 4:
+            ref = ref.at[pl.ds(way * AG_HALF, AG_HALF)]
+        n = 2 * (s - 3) + way
+        return remote(ref, ref, rel_s.at[n], rel_r.at[n], ctx_at(1 - p, z))
+
+    def agz_start(s, way, j):
+        if j == 0:
+            agz(s, way, 0, True, False).start()
+            return
+        on_plane(0, lambda: agz(s, way, 1, True, True).start())
+        if s < 3:
+            on_plane(1, lambda: agz(s, way, 1, True, False).start())
+
+    def agz_wait(s, way, j):
+        if j == 0:
+            agz(s, way, 0, False, False).wait_recv()
+            if s >= 3:
+                on_plane(0, lambda: relay(s, way).start())
+            return
+        on_plane(0, lambda: agz(s, way, 1, False, True).wait_recv())
+        on_plane(1, lambda: (agz(s, way, 1, False, False) if s < 3 else relay(s, way)).wait_recv())
+
+    def agz_sent(s, way, j):
+        if j == 0:
+            agz(s, way, 0, True, False).wait_send()
+            if s >= 3:
+                on_plane(0, lambda: relay(s, way).wait_send())
+            return
+        on_plane(0, lambda: agz(s, way, 1, True, True).wait_send())
+        if s < 3:
+            on_plane(1, lambda: agz(s, way, 1, True, False).wait_send())
+
+    def rsz(s, way, j, middle):
+        half = s == 1
+        src = snd.at[0, 0, j] if half else snd.at[s - 1, way, j]
+        dst = rcv.at[s - 1, way, j]
+        if middle:
+            n = RS_MID_N // 2 if half else RS_MID_N
+            rows = pl.ds(RS_MID + (way * n if half else 0), n)
+            src, dst = src.at[rows], dst.at[rows]
+        elif half:
+            rows = pl.ds(way * RS_HALF, RS_HALF)
+            src, dst = src.at[rows], dst.at[rows]
         return remote(src, dst, rsz_s.at[s - 1, way, j], rsz_r.at[s - 1, way, j], ctx_at(p, z + 1 - 2 * way))
 
-    def rsx():
-        return remote(xsnd, xrcv, rsx_s.at[0], rsx_r.at[0], ctx_at(1 - p, z))
+    def share(n):
+        src = snd.at[0, 0, 1] if isinstance(n, int) and n == 0 else snd.at[1, n - 1, 1]
+        return remote(src, xr.at[n], shr_s.at[n], shr_r.at[n], ctx_at(1 - p, z))
+
+    def rsz_start(s, way, j):
+        if j == 0:
+            rsz(s, way, 0, False).start()
+            return
+        on_plane(0, lambda: rsz(s, way, 1, True).start())
+        if s >= 3:
+            on_plane(1, lambda: rsz(s, way, 1, False).start())
+        elif s == 2:
+            on_plane(1, lambda: share(1 + way).start())
+
+    def rsz_wait(s, way, j):
+        if j == 0:
+            rsz(s, way, 0, False).wait_recv()
+            return
+        on_plane(0, lambda: rsz(s, way, 1, True).wait_recv())
+        if s >= 3:
+            on_plane(1, lambda: rsz(s, way, 1, False).wait_recv())
+
+    def rsz_sent(s, way, j):
+        if j == 0:
+            rsz(s, way, 0, False).wait_send()
+            return
+        on_plane(0, lambda: rsz(s, way, 1, True).wait_send())
+        if s >= 3:
+            on_plane(1, lambda: rsz(s, way, 1, False).wait_send())
+
+    def rsx(middle):
+        rows = pl.ds(RS_MID, RS_MID_N) if middle else pl.ds(0, RS_ALL)
+        return remote(xsnd.at[rows], xrcv.at[rows], rsx_s.at[0], rsx_r.at[0], ctx_at(1 - p, z))
 
     def row_copy(buf, k, n, out):
         up, down, sib = row_at(y + 1, xh, core), row_at(y - 1, xh, core), row_at(y, xh, 1 - core)
@@ -157,9 +232,10 @@
         load.wait()
     pl.semaphore_wait(barrier, NC + 2)
 
-    agx().start()
-    agz_out(1, 0, 0).start()
-    agz_out(1, 1, 0).start()
+    for plane in range(2):
+        on_plane(plane, lambda: agx(True, plane).start())
+    agz_start(1, 0, 0)
+    agz_start(1, 1, 0)
     row_stage(cot, 0, 0)
 
     qt[...] = jnp.transpose(q_ref[...].astype(F32)).astype(BF16)
@@ -177,6 +253,14 @@
         rcv[0, 0, j, RS_HALF:, :] = jnp.zeros((RS_ALL - RS_HALF, HD), BF16)
         rcv[0, 1, j, :RS_HALF, :] = jnp.zeros((RS_HALF, HD), BF16)
 
+    @pl.when(p == 1)
+    def _():
+        for way in range(2):
+            rcv[0, way, 1] = jnp.zeros((RS_ALL, HD), BF16)
+            rcv[1, way, 1] = jnp.zeros((RS_ALL, HD), BF16)
+        xr[...] = jnp.zeros_like(xr)
+        xrcv[...] = jnp.zeros_like(xrcv)
+
     def online(logits, values, m_ref, l_ref, acc_ref):
         m_old = m_ref[...]
         m_new = jnp.maximum(m_old, jnp.max(logits, axis=0, keepdims=True))
@@ -213,9 +297,10 @@
 
         @pl.when(t == 1)
         def _():
-            agx_in().wait_recv()
-            agz_out(1, 0, 1).start()
-            agz_out(1, 1, 1).start()
+            for plane in range(2):
+                on_plane(plane, lambda: agx(False, plane).wait_recv())
+            agz_start(1, 0, 1)
+            agz_start(1, 1, 1)
             row_stage(cot, 0, 1)
 
         for hop in range(1, 5):
@@ -224,9 +309,9 @@
             def _():
                 for jj in range(2):
                     for ww in range(2):
-                        agz_in(hop, ww, jj, hop == 4).wait_recv()
+                        agz_wait(hop, ww, jj)
                         if hop < 4:
-                            agz_out(hop + 1, ww, jj, hop == 3).start()
+                            agz_start(hop + 1, ww, jj)
                 if hop == 1:
                     for jj in range(1, NC):
                         w_out(jj).start()
@@ -291,9 +376,9 @@
         v = u - 2
         first, last = u < 2, u == 14
         s = jnp.where(first, 1, v // 4 + 2)
-        i = jnp.where(first, u, jnp.where(last, 1, v % 4))
+        i = jnp.where(first, 1 - u, jnp.where(last, 1, v % 4))
         way, j = i // 2, i % 2
-        slot = jnp.where(first, u, v % 4)
+        slot = jnp.where(first, 1 - u, v % 4)
         d = 5 - s
         pa = plane_of(j)
         zb = zmod((1 - 2 * way) * d)
@@ -309,26 +394,38 @@
 
         cross_backward(pa, zb, slot)
 
+        @pl.when(u == 0)
+        def _():
+            snd[0, 0, 1] = part[1].astype(BF16)
+            rsz_start(1, 0, 1)
+            rsz_start(1, 1, 1)
+            on_plane(1, lambda: share(0).start())
+
         @pl.when(u == 1)
         def _():
-            for jj in range(2):
-                snd[0, 0, jj] = part[jj].astype(BF16)
-                rsz(1, 0, jj, True).start()
-                rsz(1, 1, jj, True).start()
             row_stage(hid, 1, 1)
+            on_plane(0, lambda: share(0).wait_recv())
+            snd[0, 0, 0] = (part[0] + xr[0].astype(F32)).astype(BF16)
+            rsz_start(1, 0, 0)
+            rsz_start(1, 1, 0)
 
         for hop in range(2, 5):
 
             @pl.when(v == 4 * (hop - 2) + 3)
             def _():
-                def pass_on(n, inner):
-                    ww, jj = n // 2, n % 2
-                    rsz(hop - 1, ww, jj, hop == 2).wait_recv()
-                    snd[hop - 1, ww, jj] = (part[n] + rcv[hop - 2, ww, jj].astype(F32)).astype(BF16)
-                    rsz(hop, ww, jj).start()
-                    return inner
-
-                lax.fori_loop(0, 4, pass_on, 0)
+                for jj in (1, 0):
+
+                    def pass_on(ww, inner):
+                        rsz_wait(hop - 1, ww, jj)
+                        terms = part[2 * ww + jj] + rcv[hop - 2, ww, jj].astype(F32)
+                        if hop == 2 and jj == 0:
+                            on_plane(0, lambda: share(1 + ww).wait_recv())
+                            terms = terms + xr[1 + ww].astype(F32)
+                        snd[hop - 1, ww, jj] = terms.astype(BF16)
+                        rsz_start(hop, ww, jj)
+                        return inner
+
+                    lax.fori_loop(0, 2, pass_on, 0)
                 row_stage(hid, 1, hop)
 
         return carry
@@ -346,14 +443,16 @@
     gq_ref[...] = jnp.transpose(dq_t[...]) * SCALE
     gcq_ref[...] = jnp.transpose(dcq_t[...]) * SCALE
 
-    rsz(4, 0, 1).wait_recv()
-    rsz(4, 1, 1).wait_recv()
+    rsz_wait(4, 0, 1)
+    rsz_wait(4, 1, 1)
     xsnd[...] = (part[0] + rcv[3, 0, 1].astype(F32) + rcv[3, 1, 1].astype(F32)).astype(BF16)
-    rsx().start()
-    rsz(4, 0, 0).wait_recv()
-    rsz(4, 1, 0).wait_recv()
+    on_plane(0, lambda: rsx(True).start())
+    on_plane(1, lambda: rsx(False).start())
+    rsz_wait(4, 0, 0)
+    rsz_wait(4, 1, 0)
     part[1] = part[1] + rcv[3, 0, 0].astype(F32) + rcv[3, 1, 0].astype(F32)
-    rsx().wait_recv()
+    on_plane(0, lambda: rsx(False).wait_recv())
+    on_plane(1, lambda: rsx(True).wait_recv())
 
     def total(at, rows):
         return part[1, pl.ds(at, rows), :] + xrcv[pl.ds(at, rows), :].astype(F32)
@@ -365,13 +464,16 @@
     gw_ref[pl.ds(0, HD // 2), :] = total(GT0, HD // 2)
     gw_ref[pl.ds(HD // 2, HD // 2), :] = total(GB0, HD // 2)
 
-    agx().wait_send()
-    rsx().wait_send()
+    for plane in range(2):
+        on_plane(plane, lambda: agx(True, plane).wait_send())
+        on_plane(plane, lambda: rsx(plane == 0).wait_send())
+    for n in range(3):
+        on_plane(1, lambda: share(n).wait_send())
     for jj in range(2):
         for ww in range(2):
             for s in range(1, 5):
-                agz_out(s, ww, jj, s == 4).wait_send()
-                rsz(s, ww, jj, s == 1).wait_send()
+                agz_sent(s, ww, jj)
+                rsz_sent(s, ww, jj)
     for n in range(9):
         row_copy(cot, 0, n, True).wait_send()
         row_copy(hid, 1, n, True).wait_send()
@@ -409,8 +511,10 @@
             wide, wide, line, line, line, line, line, line,
             pltpu.VMEM((NC, T), F32),
             wide, wide,
+            pltpu.VMEM((3, RS_ALL, HD), BF16),
             dma((6,)), dma((1,)), dma((1,)), dma((4, 2, 2)), dma((4, 2, 2)), dma((4, 2, 2)), dma((4, 2, 2)),
             dma((1,)), dma((1,)), dma((2, 9)), dma((2, 9)), dma((NC,)), dma((NC,)),
+            dma((4,)), dma((4,)), dma((3,)), dma((3,)),
         ],
         compiler_params=pltpu.CompilerParams(
             collective_id=0, has_side_effects=True, vmem_limit_bytes=60 * 1024 * 1024

time: 144 us -> 131 us (0.910)
  Pallas kernels: 134 us -> 120 us
    pallas_call x1, Pallas kernels: 134 us -> 120 us  [shards(): pl.pallas_call(body, out_shape=(jax.ShapeDtypeStruct((T, HD), BF16), big,...]
where the time goes in v2:
time: 131 us; the launch traced here: 130 us
  Pallas kernels  120 us (92%)
  local copies, waits for them, and re-layouts  9.51 us (7%)
    pallas_call x1, Pallas kernels, shards(): pl.pallas_call(body, out_shape=(jax.ShapeDtypeStruct((T, HD), BF16), big,...  120 us
    unnamed x23, local copies, waits for them, and re-layouts  9.51 us

profile of v2, /device:TPU:8, one launch (start us, length us, event | category | flops | bytes accessed | tf_op | source)
XLA Modules:
  0.0 130.2 jit_solution(8617441868767820871)
XLA Ops:
  0.6 1.6 %copy.17.inc_ref = s32[512,4]{1,0:T(8,128)} copy(s32[512,4]{0,1:T(4,128)} %param.15) | data formatting | bytes 16384 | tf_op args[6]
  2.2 120.1 %attention_layer.1 = (bf16[512,128]{1,0:T(8,128)(2,1)}, f32[512,128]{1,0:T(8,128)}, f32[512,128]{1,0:T(8,128)}, f32[512,128]{1,0:T(8,128)}, f32[512,128]{1,0:T(8...) custom-call(bf16[512,128]{1,0:T(8,128)(2,1)} %q_ref.1, bf16[512,128]{1,0:T(8,128)(2,1)} %cq_ref.1, ...), custom_call_target="tpu_custom_call" | custom-call | tf_op jit(solution)/shard_map/attention_layer/pallas_call | solution.py:491
  122.2 0.0 copy-start.3
  122.3 1.6 %copy.26 = bf16[512,128]{1,0:T(8,128)(2,1)} copy(bf16[512,128]{1,0:T(8,128)(2,1)} %get-tuple-element.16) | data formatting | bytes 262144
  123.9 0.0 copy-done.3
  123.9 0.0 copy-start.2
  123.9 0.7 copy.27
  124.6 0.3 copy-done.2
  124.9 0.0 copy-start.1
  124.9 0.7 copy.28
  125.6 0.3 copy-done.1
  126.0 0.0 copy-start
  126.0 0.7 copy.29
  126.7 0.3 copy-done
  127.0 0.0 copy-start.6
  127.0 0.7 copy.30
  127.7 0.2 copy-done.6
  127.9 0.0 copy-start.5
  127.9 0.6 copy.31
  128.5 0.2 copy-done.5
  128.7 0.0 copy-start.4
  128.7 0.6 copy.32
  129.4 0.2 copy-done.4
  129.6 0.6 copy.33
Async XLA Ops:
  122.2 1.6 %copy-start.3 = (f32[512,128]{1,0:T(8,128)S(1)}, f32[512,128]{1,0:T(8,128)}, u32[]{:S(2)}) copy-start(f32[512,128]{1,0:T(8,128)} %get-tuple-element.17) | copy-start | bytes 786436
  123.9 1.0 copy-start.2
  124.9 1.0 copy-start.1
  126.0 1.0 copy-start
  127.0 0.9 copy-start.6
  127.9 0.9 copy-start.5
  128.7 0.9 copy-start.4

commit v3 on v2

--- a/solution.py
+++ b/solution.py
@@ -289,11 +289,19 @@
     self_forward(p, z, True)
     cross_forward(p, z)
 
+    def hidden_grad():
+        grad = jnp.zeros((T, HD), F32)
+        for n in range(NC):
+            grad = grad + nt(cot[n // 4, n % 2, (n // 2) % 2], w_ref[:, n * HD : (n + 1) * HD])
+        grad = grad.astype(BF16)
+        do_ref[...] = grad
+        dot_t[...] = jnp.transpose(grad.astype(F32)).astype(BF16)
+
     def forward_step(t, carry):
         v = t - 2
         s = jnp.where(t < 2, 0, v // 4 + 1)
         i = jnp.where(t < 2, 1, v % 4)
-        way, j = i // 2, i % 2
+        way, j = jnp.where(s == 3, i % 2, i // 2), jnp.where(s == 3, i // 2, i % 2)
 
         @pl.when(t == 1)
         def _():
@@ -303,20 +311,32 @@
             agz_start(1, 1, 1)
             row_stage(cot, 0, 1)
 
+        def arrive(hop, jj):
+            for ww in range(2):
+                agz_wait(hop, ww, jj)
+                if hop < 4:
+                    agz_start(hop + 1, ww, jj)
+
         for hop in range(1, 5):
 
             @pl.when(v == 4 * (hop - 1))
             def _():
-                for jj in range(2):
-                    for ww in range(2):
-                        agz_wait(hop, ww, jj)
-                        if hop < 4:
-                            agz_start(hop + 1, ww, jj)
+                arrive(hop, 0)
+                if hop < 3:
+                    arrive(hop, 1)
                 if hop == 1:
                     for jj in range(1, NC):
                         w_out(jj).start()
-                if hop > 1:
-                    row_stage(cot, 0, hop)
+                if hop < 4:
+                    row_stage(cot, 0, hop + 1)
+                if hop == 3:
+                    hidden_grad()
+
+            if hop > 2:
+
+                @pl.when(v == (10 if hop == 3 else 13))
+                def _():
+                    arrive(hop, 1)
 
         pa = plane_of(j)
         zb = zmod((2 * way - 1) * s)
@@ -330,13 +350,7 @@
 
     lax.fori_loop(1, NC, forward_step, 0)
 
-    grad = jnp.zeros((T, HD), F32)
-    for n in range(NC):
-        grad = grad + nt(cot[n // 4, n % 2, (n // 2) % 2], w_ref[:, n * HD : (n + 1) * HD])
-    grad = grad.astype(BF16)
-    do_ref[...] = grad
-    grad_t = jnp.transpose(grad.astype(F32))
-    dot_t[...] = grad_t.astype(BF16)
+    grad_t = dot_t[...].astype(F32)
     out_s = acc_s[...] / l_s[...]
     out_c = acc_c[...] / l_c[...]
     hidden_t = out_s + out_c
@@ -376,9 +390,10 @@
         v = u - 2
         first, last = u < 2, u == 14
         s = jnp.where(first, 1, v // 4 + 2)
-        i = jnp.where(first, 1 - u, jnp.where(last, 1, v % 4))
-        way, j = i // 2, i % 2
-        slot = jnp.where(first, 1 - u, v % 4)
+        i = v % 4
+        way = jnp.where(first | last, 0, i % 2)
+        j = jnp.where(first, 1 - u, jnp.where(last, 1, 1 - i // 2))
+        slot = jnp.where(last, 0, 2 * way + j)
         d = 5 - s
         pa = plane_of(j)
         zb = zmod((1 - 2 * way) * d)
@@ -409,23 +424,28 @@
             rsz_start(1, 0, 0)
             rsz_start(1, 1, 0)
 
+        def pass_on(hop, jj):
+            def one(ww, inner):
+                rsz_wait(hop - 1, ww, jj)
+                terms = part[2 * ww + jj] + rcv[hop - 2, ww, jj].astype(F32)
+                if hop == 2 and jj == 0:
+                    on_plane(0, lambda: share(1 + ww).wait_recv())
+                    terms = terms + xr[1 + ww].astype(F32)
+                snd[hop - 1, ww, jj] = terms.astype(BF16)
+                rsz_start(hop, ww, jj)
+                return inner
+
+            lax.fori_loop(0, 2, one, 0)
+
         for hop in range(2, 5):
+
+            @pl.when(v == 4 * (hop - 2) + 1)
+            def _():
+                pass_on(hop, 1)
 
             @pl.when(v == 4 * (hop - 2) + 3)
             def _():
-                for jj in (1, 0):
-
-                    def pass_on(ww, inner):
-                        rsz_wait(hop - 1, ww, jj)
-                        terms = part[2 * ww + jj] + rcv[hop - 2, ww, jj].astype(F32)
-                        if hop == 2 and jj == 0:
-                            on_plane(0, lambda: share(1 + ww).wait_recv())
-                            terms = terms + xr[1 + ww].astype(F32)
-                        snd[hop - 1, ww, jj] = terms.astype(BF16)
-                        rsz_start(hop, ww, jj)
-                        return inner
-
-                    lax.fori_loop(0, 2, pass_on, 0)
+                pass_on(hop, 0)
                 row_stage(hid, 1, hop)
 
         return carry

time: 131 us -> 128 us (0.977)
  Pallas kernels: 120 us -> 117 us
    pallas_call x1, Pallas kernels: 120 us -> 117 us  [shards(): pl.pallas_call(body, out_shape=(jax.ShapeDtypeStruct((T, HD), BF16), big,...]
where the time goes in v3:
time: 128 us; the launch traced here: 127 us
  Pallas kernels  117 us (91%)
  local copies, waits for them, and re-layouts  9.51 us (7%)
    pallas_call x1, Pallas kernels, shards(): pl.pallas_call(body, out_shape=(jax.ShapeDtypeStruct((T, HD), BF16), big,...  117 us
    unnamed x23, local copies, waits for them, and re-layouts  9.51 us

profile of v3, /device:TPU:8, one launch (start us, length us, event | category | flops | bytes accessed | tf_op | source)
XLA Modules:
  0.0 127.4 jit_solution(13639619124649170511)
XLA Ops:
  0.6 1.6 %copy.17.inc_ref = s32[512,4]{1,0:T(8,128)} copy(s32[512,4]{0,1:T(4,128)} %param.15) | data formatting | bytes 16384 | tf_op args[6]
  2.2 117.2 %attention_layer.1 = (bf16[512,128]{1,0:T(8,128)(2,1)}, f32[512,128]{1,0:T(8,128)}, f32[512,128]{1,0:T(8,128)}, f32[512,128]{1,0:T(8,128)}, f32[512,128]{1,0:T(8...) custom-call(bf16[512,128]{1,0:T(8,128)(2,1)} %q_ref.1, bf16[512,128]{1,0:T(8,128)(2,1)} %cq_ref.1, ...), custom_call_target="tpu_custom_call" | custom-call | tf_op jit(solution)/shard_map/attention_layer/pallas_call | solution.py:511
  119.4 0.0 copy-start.3
  119.4 1.6 %copy.26 = bf16[512,128]{1,0:T(8,128)(2,1)} copy(bf16[512,128]{1,0:T(8,128)(2,1)} %get-tuple-element.16) | data formatting | bytes 262144
  121.0 0.0 copy-done.3
  121.0 0.0 copy-start.2
  121.0 0.7 copy.27
  121.7 0.3 copy-done.2
  122.1 0.0 copy-start.1
  122.1 0.7 copy.28
  122.8 0.3 copy-done.1
  123.1 0.0 copy-start
  123.1 0.7 copy.29
  123.8 0.3 copy-done
  124.2 0.0 copy-start.6
  124.2 0.7 copy.30
  124.9 0.2 copy-done.6
  125.0 0.0 copy-start.5
  125.0 0.6 copy.31
  125.7 0.2 copy-done.5
  125.9 0.0 copy-start.4
  125.9 0.6 copy.32
  126.5 0.2 copy-done.4
  126.8 0.6 copy.33
Async XLA Ops:
  119.4 1.6 %copy-start.3 = (f32[512,128]{1,0:T(8,128)S(1)}, f32[512,128]{1,0:T(8,128)}, u32[]{:S(2)}) copy-start(f32[512,128]{1,0:T(8,128)} %get-tuple-element.17) | copy-start | bytes 786436
  121.0 1.0 copy-start.2
  122.1 1.0 copy-start.1
  123.1 1.0 copy-start
  124.2 0.9 copy-start.6
  125.0 0.9 copy-start.5
  125.9 0.9 copy-start.4
